TPU v7x, 256 devices: a whole 4x4x8 slice. The times are simulated.
256 devices in a mesh: band: 4 (over x), dom: 64 (over z, y, core).
Axes of the slice: x: 4, y: 4, z: 8, core: 2. Of those that a mesh axis runs over, the one named last changes fastest.
Arguments:
- orbitals: bfloat16 [256, 512, 2048], P('dom', None, 'band'), may hold values from -6 to 6
- projector_blocks: bfloat16 [4, 64, 96, 256, 128], P('band', 'dom'), may hold values from -0.1875 to 0.1875
- block_rows: int32 [4, 64, 96], P('band', 'dom'), may hold values from 0 to 15, as said below
- block_cols: int32 [4, 64, 96], P('band', 'dom'), may hold values from 0 to 26
- block_counts: int32 [4, 64], P('band', 'dom'), may hold values from 16 to 96, as said below
- strengths: float32 [73728], P('dom'), may hold values from -1.5 to 1.5
Outputs:
- applied: bfloat16 [256, 512, 2048], P('dom', None, 'band')
Inputs may be any that keep to these rules, and one draw needn't show every extreme that they name: `block_rows`: the slots of one device name distinct pairs of row block and column block. `block_counts`: some device has all 96 slots live.
All inputs are finite; a program needn't handle non-finite values.
Results may differ from a plain program's by a relative error of at most 0.0049.
Values may be sent and summed in bfloat16 or wider, within the bound.
A program may use at most 128 MiB of HBM per device.

v0:
```python
import jax
import jax.numpy as jnp
from jax import lax
from jax.sharding import PartitionSpec as P


def passed_along(value, axis, steps):
    count = lax.axis_size(axis)
    pairs = [(source, (source + steps) % count) for source in range(count)]
    return lax.ppermute(value, axis, pairs)


def padded(shard, sides, width):
    for axis, dim in sides:
        size, length = (lax.axis_size(axis), shard.shape[dim])
        up = [(i, (i + 1) % size) for i in range(size)]
        down = [(j, i) for i, j in up]
        last = lax.slice_in_dim(shard, length - width, length, axis=dim)
        leading = lax.slice_in_dim(shard, 0, width, axis=dim)
        before = lax.ppermute(last, axis, up)
        after = lax.ppermute(leading, axis, down)
        shard = jnp.concatenate([before, shard, after], axis=dim)
    return shard


def per_device(orbitals, projector_blocks, block_rows, block_cols, block_counts, strengths):
    slab_states = lax.all_to_all(orbitals, "dom", split_axis=1, concat_axis=0, tiled=True)
    state_total = slab_states.shape[0]
    planes = slab_states.shape[1]
    points = slab_states.shape[2]
    weights = projector_blocks[0, 0]
    slot_total = weights.shape[0]
    row_width = weights.shape[1]
    col_width = weights.shape[2]
    row_blocks = planes * points // row_width
    col_blocks = strengths.shape[0] // col_width
    slot_rows = block_rows[0, 0]
    slot_cols = block_cols[0, 0]
    live_total = block_counts[0, 0]
    live_weight = (jnp.arange(slot_total, dtype=jnp.int32) < live_total).astype(jnp.float32)
    picked = jnp.take(slab_states.reshape(state_total, row_blocks, row_width), slot_rows, axis=1)
    projected = jnp.einsum("skr,krc->kcs", picked, weights, preferred_element_type=jnp.float32)
    projected = projected * live_weight[:, None, None]
    partial_value = (
        jnp.zeros((3 * col_blocks, col_width, state_total), jnp.float32)
        .at[slot_cols]
        .add(projected)
    )
    partial_value = partial_value.reshape(3, col_blocks, col_width, state_total)
    scaling = strengths.reshape(col_blocks, col_width, 1)
    summed = lax.psum(partial_value, "band")
    below_part = passed_along(summed[2], "dom", 1)
    above_part = passed_along(summed[0], "dom", -1)
    scaled = (scaling * (summed[1] + below_part + above_part)).astype(jnp.bfloat16)
    neighbours = padded(scaled[None], (("dom", 0),), 1)
    neighbours = neighbours.reshape(3 * col_blocks, col_width, state_total)
    selected = jnp.take(neighbours, slot_cols, axis=0)
    returned = jnp.einsum("krc,kcs->skr", weights, selected, preferred_element_type=jnp.float32)
    returned = returned * live_weight[None, :, None]
    placed = (
        jnp.zeros((state_total, row_blocks, row_width), jnp.float32)
        .at[:, slot_rows, :]
        .add(returned)
    )
    result = placed.astype(jnp.bfloat16).reshape(state_total, planes, points)
    return lax.all_to_all(result, "dom", split_axis=0, concat_axis=1, tiled=True)


def solution(mesh):
    return jax.shard_map(
        per_device,
        mesh=mesh,
        in_specs=(
            P("dom", None, "band"),
            P("band", "dom", None, None, None),
            P("band", "dom", None),
            P("band", "dom", None),
            P("band", "dom"),
            P("dom"),
        ),
        out_specs=P("dom", None, "band"),
        check_vma=False,
    )
```

profile of v0, /device:TPU:8, one launch (start us, length us, event | category | flops | bytes accessed | tf_op | source)
XLA Modules:
  0.0 411.5 jit_solution(6211134194385298743)
XLA Ops:
  6.5 0.0 copy-start.4
  6.5 0.0 copy-start.5
  6.5 4.6 %copy.21 = bf16[4,512,512]{2,0,1:T(4,128)(2,1)} copy(bf16[4,512,512]{2,1,0:T(8,128)(2,1)} %param.6) | data formatting | bytes 4194304 | tf_op args[0]
  11.1 12.1 %all-to-all-start = ((bf16[4,512,512]{2,0,1:T(4,128)(2,1)}), bf16[4,512,512]{2,0,1:T(4,128)(2,1)S(1)}, u32[]{:S(2)}, u32[]{:S(2)}) async-start(bf16[4,512,512]{2,0,1:T(4,128)(2,1)} %copy.21), calls=%async_computation | async-start | bytes 4194304 | tf_op jit(solution)/shard_map/all_to_all | solution.py:27
  23.2 0.0 all-reduce.2.cloned.1.call-start
  23.9 0.0 copy-done.4
  23.9 0.0 copy-start.2
  23.9 0.0 copy-done.5
  24.0 0.5 copy-done.2
  24.5 50.0 %all-to-all-done = bf16[4,512,512]{2,0,1:T(4,128)(2,1)S(1)} async-done(((bf16[4,512,512]{2,0,1:T(4,128)(2,1)}), bf16[4,512,512]{2,0,1:T(4,128)(2,1)S(1)}, u32[]{:S(2)}, u32[]{:S(2)}) %all-to-all-start) | async-done | bytes 2097184 | tf_op jit(solution)/shard_map/all_to_all | solution.py:27
  74.5 1.9 copy.33
  76.4 4.1 reshape.93
  80.5 2.3 copy.23
  82.8 6.8 %gather_fusion = bf16[96,256,256]{2,1,0:T(8,128)(2,1)} fusion(bf16[256,16,256]{2,0,1:T(8,128)(2,1)S(1)} %copy.23, s32[1024]{0:T(1024)S(1)} %pad_clamp_fusion.1), kind=kCustom, calls=%fused_computation | custom fusion | bytes 25166208 | tf_op jit(solution)/shard_map/jit(_take)/gather | solution.py:41
  89.5 14.4 %multiply_bitcast_fusion = f32[96,128,256]{1,2,0:T(8,128)} fusion(f32[96]{0:T(128)S(1)} %get-tuple-element.7, bf16[1,1,96,256,128]{4,3,2,1,0:T(8,128)(2,1)} %param.7, bf16[96,256,256]{2,1,0:T(8,128)(2,1)} %gather_fusion, pred[96]{0:T(512)(128)(4,1)S(1)} %get-tuple-element.8), kind=kOutput, calls=%fused_computation.8 | convolution fusion | flops 1620049920 | bytes 31457760 | tf_op jit(solution)/shard_map/skr,krc->kcs/dot_general | solution.py:42
  103.9 12.6 %copy.24 = f32[96,128,256]{2,1,0:T(8,128)} copy(f32[96,128,256]{1,2,0:T(8,128)} %multiply_bitcast_fusion) | data formatting | bytes 25165824 | tf_op jit(solution)/shard_map/mul | solution.py:43
  116.5 0.4 broadcast_in_dim.35
  116.9 18.4 %scatter_fusion = f32[27,128,256]{2,1,0:T(8,128)S(1)} fusion(f32[27,128,256]{2,1,0:T(8,128)S(1)} %broadcast_in_dim.35, s32[96]{0:T(128)S(1)} %fusion.23, f32[96,128,256]{2,1,0:T(8,128)} %copy.24), kind=kCustom, calls=%fused_computation.2 | custom fusion | flops 3145728 | bytes 37749120 | tf_op jit(solution)/shard_map/scatter-add | solution.py:47
  135.3 0.0 copy-start
  135.3 0.0 copy-start.1
  135.4 1.8 copy-done
  137.1 0.0 all-reduce.2.cloned.1.call-update
  137.2 0.0 copy-start.6
  137.2 83.6 %all-reduce.2.cloned.1.call-done = f32[3,9,128,256]{3,2,1,0:T(8,128)} async-done(((f32[3,9,128,256]{3,2,1,0:T(8,128)}), f32[3,9,128,256]{3,2,1,0:T(8,128)}) %all-reduce.2.cloned.1.call-update) | async-done | bytes 3538960 | tf_op jit(solution)/shard_map/psum | solution.py:51
  220.8 1.8 slice_bitcast_fusion.1
  222.6 0.3 collective-permute-start
  222.9 1.7 collective-permute-start.1
  224.6 13.9 %collective-permute-done = f32[9,128,256]{2,1,0:T(8,128)S(1)} collective-permute-done((f32[9,128,256]{2,1,0:T(8,128)S(1)}, f32[9,128,256]{2,1,0:T(8,128)S(1)}, u32[]{:S(2)}, u32[]{:S(2)}) %collective-permute-start) | collective-permute-done | bytes 1179680 | tf_op jit(solution)/shard_map/ppermute | solution.py:10
  238.5 0.0 collective-permute-done.1
  238.5 0.0 copy-done.1
  238.5 1.6 fusion.21
  240.1 1.7 collective-permute-start.2
  241.8 0.5 collective-permute-start.3
  242.3 0.0 copy-done.6
  242.3 7.5 %collective-permute-done.2 = bf16[1,9,128,256]{3,2,1,0:T(8,128)(2,1)S(1)} collective-permute-done((bf16[1,9,128,256]{3,2,1,0:T(8,128)(2,1)S(1)}, bf16[1,9,128,256]{3,2,1,0:T(8,128)(2,1)S(1)}, u32[]{:S(2)}, u32[]{:S(2)}) %collective-permute-start.2) | collective-permute-done | bytes 589856 | tf_op jit(solution)/shard_map/ppermute | solution.py:20
  249.8 0.0 collective-permute-done.3
  249.8 0.2 pad_maximum_fusion
  250.0 6.1 %gather_fusion.1 = bf16[96,128,256]{2,1,0:T(8,128)(2,1)} fusion(bf16[27,128,256]{2,1,0:T(8,128)(2,1)S(1)} %bitcast.65, s32[1024]{0:T(1024)S(1)} %pad_clamp_fusion), kind=kCustom, calls=%fused_computation.1 | custom fusion | bytes 12583296 | tf_op jit(solution)/shard_map/jit(_take)/gather | solution.py:57
  256.0 14.3 %broadcast_multiply_fusion = f32[96,256,256]{2,1,0:T(8,128)} fusion(f32[96]{0:T(128)S(1)} %get-tuple-element.7, bf16[1,1,96,256,128]{4,3,2,1,0:T(8,128)(2,1)} %param.7, bf16[96,128,256]{2,1,0:T(8,128)(2,1)} %gather_fusion.1, pred[96]{0:T(512)(128)(4,1)S(1)} %compare_and_fusion.1), kind=kOutput, calls=%fused_computation.7 | convolution fusion | flops 1620049920 | bytes 37749216 | tf_op jit(solution)/shard_map/krc,kcs->skr/dot_general | solution.py:58
  270.3 0.0 copy-start.3
  270.3 2.4 broadcast_in_dim.33
  272.7 0.0 copy-done.3
  272.7 54.2 %scatter_fusion.1 = f32[256,16,256]{2,0,1:T(8,128)} fusion(f32[256,16,256]{2,0,1:T(8,128)} %broadcast_in_dim.33, s32[96]{0:T(128)S(1)} %copy-done.3, f32[96,256,256]{2,1,0:T(8,128)} %broadcast_multiply_fusion), kind=kCustom, calls=%fused_computation.3 | custom fusion | flops 6291456 | bytes 75497856 | tf_op jit(solution)/shard_map/scatter-add | solution.py:63
  327.0 2.4 convert_element_type.19
  329.4 2.4 copy.26
  331.8 3.4 copy.27
  335.2 68.0 %all_to_all.33 = bf16[256,8,512]{2,1,0:T(8,128)(2,1)S(1)} all-to-all(bf16[256,8,512]{2,1,0:T(8,128)(2,1)S(1)} %copy.27), channel_id=1, replica_groups=mesh['band'=4,'dom'=64] {'dom'}, dimensions={0} | all-to-all | bytes 4194304 | tf_op jit(solution)/shard_map/all_to_all | solution.py:66
  403.1 1.5 copy.32
  (6 shorter events, 0.0 us)
Async XLA Ops:
  6.5 17.4 %copy-start.4 = (s32[1,1,96]{2,1,0:T(1,128)S(1)}, s32[1,1,96]{2,1,0:T(1,128)}, u32[]{:S(2)}) copy-start(s32[1,1,96]{2,1,0:T(1,128)} %param.8) | copy-start | bytes 1156
  6.5 17.4 %copy-start.5 = (s32[1,1,96]{2,1,0:T(1,128)S(1)}, s32[1,1,96]{2,1,0:T(1,128)}, u32[]{:S(2)}) copy-start(s32[1,1,96]{2,1,0:T(1,128)} %param.9) | copy-start | bytes 1156
  11.1 63.4 %all-to-all-start = ((bf16[4,512,512]{2,0,1:T(4,128)(2,1)}), bf16[4,512,512]{2,0,1:T(4,128)(2,1)S(1)}, u32[]{:S(2)}, u32[]{:S(2)}) async-start(bf16[4,512,512]{2,0,1:T(4,128)(2,1)} %copy.21), calls=%async_computation | async-start | bytes 4194304 | tf_op jit(solution)/shard_map/all_to_all | solution.py:27
  23.2 197.6 %all-reduce.2.cloned.1.call-start = ((), (), s32[]{:S(2)}) async-start(), calls=%async_computation.2 | async-start | bytes 7077888 | tf_op jit(solution)/shard_map/psum | solution.py:51
  23.9 0.6 copy-start.2
  135.3 1.8 copy-start
  135.3 103.2 %copy-start.1 = (f32[1152]{0:T(1024)S(1)}, f32[1152]{0:T(1024)}, u32[]{:S(2)}) copy-start(f32[1152]{0:T(1024)} %param.11) | copy-start | bytes 13828
  137.2 105.1 %copy-start.6 = (s32[1,1,96]{2,1,0:T(1,128)S(1)}, s32[1,1,96]{2,1,0:T(1,128)}, u32[]{:S(2)}) copy-start(s32[1,1,96]{2,1,0:T(1,128)} %param.9) | copy-start | bytes 1156
  222.6 15.9 %collective-permute-start = (f32[9,128,256]{2,1,0:T(8,128)S(1)}, f32[9,128,256]{2,1,0:T(8,128)S(1)}, u32[]{:S(2)}, u32[]{:S(2)}) collective-permute-start(f32[9,128,256]{2,1,0:T(8,128)S(1)} %get-tuple-element.5), channel_id=1, source_target_pairs={{0,1},{1,2},{2,3},{3,4},{4,5},{5,6},{6,7},{7,8},{8,9},{9,10},{10,1... | collective-permute-start | bytes 3538952 | tf_op jit(solution)/shard_map/ppermute | solution.py:10
  222.9 15.6 %collective-permute-start.1 = (f32[9,128,256]{2,1,0:T(8,128)S(1)}, f32[9,128,256]{2,1,0:T(8,128)S(1)}, u32[]{:S(2)}, u32[]{:S(2)}) collective-permute-start(f32[9,128,256]{2,1,0:T(8,128)S(1)} %get-tuple-element.6), channel_id=1, source_target_pairs={{0,63},{1,0},{2,1},{3,2},{4,3},{5,4},{6,5},{7,6},{8,7},{9,8},{10,9... | collective-permute-start | bytes 3538952 | tf_op jit(solution)/shard_map/ppermute | solution.py:10
  240.1 9.7 %collective-permute-start.2 = (bf16[1,9,128,256]{3,2,1,0:T(8,128)(2,1)S(1)}, bf16[1,9,128,256]{3,2,1,0:T(8,128)(2,1)S(1)}, u32[]{:S(2)}, u32[]{:S(2)}) collective-permute-start(bf16[1,9,128,256]{3,2,1,0:T(8,128)(2,1)S(1)} %fusion.21), channel_id=1, source_target_pairs={{0,1},{1,2},{2,3},{3,4},{4,5},{5,6},{6,7},{7,8},{8,9},{9,10},{10,1... | collective-permute-start | bytes 1769480 | tf_op jit(solution)/shard_map/ppermute | solution.py:20
  241.8 8.0 %collective-permute-start.3 = (bf16[1,9,128,256]{3,2,1,0:T(8,128)(2,1)S(1)}, bf16[1,9,128,256]{3,2,1,0:T(8,128)(2,1)S(1)}, u32[]{:S(2)}, u32[]{:S(2)}) collective-permute-start(bf16[1,9,128,256]{3,2,1,0:T(8,128)(2,1)S(1)} %fusion.21), channel_id=1, source_target_pairs={{1,0},{2,1},{3,2},{4,3},{5,4},{6,5},{7,6},{8,7},{9,8},{10,9},{11,1... | collective-permute-start | bytes 1769480 | tf_op jit(solution)/shard_map/ppermute | solution.py:21
  270.3 2.4 copy-start.3
Sparse Core Ops, SparseCore 0:
  137.3 83.4 all-reduce.1
where the time goes:
time: 412 us
  waiting for transfers between devices  155 us (38%)
  other arithmetic  76.9 us (19%)
  blocking collectives  68 us (17%)
  local copies, waits for them, and re-layouts  52.5 us (13%)
  matrix products  28.7 us (7%)
  starting transfers between devices  16.3 us (4%)
  between operations  14.2 us (3%)
    psum x1, waiting for transfers between devices, per_device(): summed = lax.psum(partial_value, 'band')  83.6 us
    all_to_all x1, blocking collectives, per_device(): lax.all_to_all(result, 'dom', split_axis=0, concat_axis=1, tiled=True)  68 us
    scatter-add x1, other arithmetic, per_device(): placed = jnp.zeros((state_total, row_blocks, row_width), jnp.float32).at[...  54.2 us
    all_to_all x1, waiting for transfers between devices, per_device(): lax.all_to_all(orbitals, 'dom', split_axis=1, concat_axis=0, tiled=True)  50 us
    scatter-add x1, other arithmetic, per_device(): partial_value = jnp.zeros((3 * col_blocks, col_width, state_total), jnp.f...  18.4 us
    dot_general x1, matrix products, per_device(): jnp.einsum('skr,krc->kcs', picked, weights, preferred_element_type=jnp.fl...  14.4 us
    dot_general x1, matrix products, per_device(): jnp.einsum('krc,kcs->skr', weights, selected, preferred_element_type=jnp....  14.3 us
    ppermute x2, waiting for transfers between devices, passed_along(): return lax.ppermute(value, axis, pairs)  13.9 us
  transfers between devices with their start and end apart: 6, of which 4 were waited for; matrix products, arithmetic and copies ran while one was open for 0% of the time, Pallas kernels for 0%

commit v1 on v0

--- a/solution.py
+++ b/solution.py
@@ -48,7 +48,7 @@
     )
     partial_value = partial_value.reshape(3, col_blocks, col_width, state_total)
     scaling = strengths.reshape(col_blocks, col_width, 1)
-    summed = lax.psum(partial_value, "band")
+    summed = jnp.sum(lax.all_gather(partial_value, "band"), axis=0)
     below_part = passed_along(summed[2], "dom", 1)
     above_part = passed_along(summed[0], "dom", -1)
     scaled = (scaling * (summed[1] + below_part + above_part)).astype(jnp.bfloat16)

time: 412 us -> 464 us (1.13)
  waiting for transfers between devices: 155 us -> 203 us
  other arithmetic: 76.9 us -> 82.4 us
    all_gather x0 -> x1, waiting for transfers between devices: none -> 131 us  [per_device(): summed = jnp.sum(lax.all_gather(partial_value, 'band'), axis=0)]
    psum x1 -> x0, waiting for transfers between devices: 83.6 us -> none  [per_device(): summed = lax.psum(partial_value, 'band')]
    reduce_sum x0 -> x1, other arithmetic: none -> 6.71 us  [per_device(): summed = jnp.sum(lax.all_gather(partial_value, 'band'), axis=0)]
where the time goes in v1:
time: 464 us; the launch traced here: 463 us
  waiting for transfers between devices  203 us (44%)
  other arithmetic  82.4 us (18%)
  blocking collectives  68.2 us (15%)
  local copies, waits for them, and re-layouts  50.3 us (11%)
  matrix products  28.7 us (6%)
  starting transfers between devices  16.3 us (4%)
  between operations  14.2 us (3%)
    all_gather x1, waiting for transfers between devices, per_device(): summed = jnp.sum(lax.all_gather(partial_value, 'band'), axis=0)  131 us
    all_to_all x1, blocking collectives, per_device(): lax.all_to_all(result, 'dom', split_axis=0, concat_axis=1, tiled=True)  68.2 us
    scatter-add x1, other arithmetic, per_device(): placed = jnp.zeros((state_total, row_blocks, row_width), jnp.float32).at[...  54.3 us
    all_to_all x1, waiting for transfers between devices, per_device(): lax.all_to_all(orbitals, 'dom', split_axis=1, concat_axis=0, tiled=True)  50.3 us
    scatter-add x1, other arithmetic, per_device(): partial_value = jnp.zeros((3 * col_blocks, col_width, state_total), jnp.f...  18.4 us
    dot_general x1, matrix products, per_device(): jnp.einsum('skr,krc->kcs', picked, weights, preferred_element_type=jnp.fl...  14.4 us
    dot_general x1, matrix products, per_device(): jnp.einsum('krc,kcs->skr', weights, selected, preferred_element_type=jnp....  14.3 us
    ppermute x2, waiting for transfers between devices, passed_along(): return lax.ppermute(value, axis, pairs)  13.9 us
  transfers between devices with their start and end apart: 6, of which 4 were waited for; matrix products, arithmetic and copies ran while one was open for 0% of the time, Pallas kernels for 0%

profile of v1, /device:TPU:8, one launch (start us, length us, event | category | flops | bytes accessed | tf_op | source)
XLA Modules:
  0.0 462.6 jit_solution(10376801089242439904)
XLA Ops:
  6.5 0.0 copy-start.2
  6.5 0.0 copy-start.3
  6.5 4.6 copy.21
  11.1 12.1 %all-to-all-start = ((bf16[4,512,512]{2,0,1:T(4,128)(2,1)}), bf16[4,512,512]{2,0,1:T(4,128)(2,1)S(1)}, u32[]{:S(2)}, u32[]{:S(2)}) async-start(bf16[4,512,512]{2,0,1:T(4,128)(2,1)} %copy.21), calls=%async_computation | async-start | bytes 4194304 | tf_op jit(solution)/shard_map/all_to_all | solution.py:27
  23.2 0.2 all-gather.2.cloned.1.call-start
  24.1 0.0 copy-done.2
  24.1 0.0 copy-done.3
  24.2 50.3 %all-to-all-done = bf16[4,512,512]{2,0,1:T(4,128)(2,1)S(1)} async-done(((bf16[4,512,512]{2,0,1:T(4,128)(2,1)}), bf16[4,512,512]{2,0,1:T(4,128)(2,1)S(1)}, u32[]{:S(2)}, u32[]{:S(2)}) %all-to-all-start) | async-done | bytes 2097184 | tf_op jit(solution)/shard_map/all_to_all | solution.py:27
  74.5 1.9 copy.33
  76.4 4.1 reshape.90
  80.5 2.3 copy.23
  82.8 6.8 %gather_fusion = bf16[96,256,256]{2,1,0:T(8,128)(2,1)} fusion(bf16[256,16,256]{2,0,1:T(8,128)(2,1)S(1)} %copy.23, s32[1024]{0:T(1024)S(1)} %pad_clamp_fusion.1), kind=kCustom, calls=%fused_computation | custom fusion | bytes 25166208 | tf_op jit(solution)/shard_map/jit(_take)/gather | solution.py:41
  89.5 14.4 %multiply_bitcast_fusion = f32[96,128,256]{1,2,0:T(8,128)} fusion(f32[96]{0:T(128)S(1)} %get-tuple-element.7, bf16[1,1,96,256,128]{4,3,2,1,0:T(8,128)(2,1)} %param.7, bf16[96,256,256]{2,1,0:T(8,128)(2,1)} %gather_fusion, pred[96]{0:T(512)(128)(4,1)S(1)} %get-tuple-element.8), kind=kOutput, calls=%fused_computation.8 | convolution fusion | flops 1620049920 | bytes 31457760 | tf_op jit(solution)/shard_map/skr,krc->kcs/dot_general | solution.py:42
  103.9 12.6 %copy.24 = f32[96,128,256]{2,1,0:T(8,128)} copy(f32[96,128,256]{1,2,0:T(8,128)} %multiply_bitcast_fusion) | data formatting | bytes 25165824 | tf_op jit(solution)/shard_map/mul | solution.py:43
  116.5 0.4 broadcast_in_dim.35
  116.9 18.4 %scatter_fusion = f32[27,128,256]{2,1,0:T(8,128)S(1)} fusion(f32[27,128,256]{2,1,0:T(8,128)S(1)} %broadcast_in_dim.35, s32[96]{0:T(128)S(1)} %fusion.23, f32[96,128,256]{2,1,0:T(8,128)} %copy.24), kind=kCustom, calls=%fused_computation.2 | custom fusion | flops 3145728 | bytes 37749120 | tf_op jit(solution)/shard_map/scatter-add | solution.py:47
  135.4 0.0 copy-start
  135.4 1.7 copy-done
  137.1 0.0 all-gather.2.cloned.1.call-update
  137.1 130.9 %all-gather.2.cloned.1.call-done = f32[4,3,9,128,256]{4,3,2,1,0:T(8,128)} async-done(((f32[1,3,9,128,256]{4,3,2,1,0:T(8,128)}), f32[4,3,9,128,256]{4,3,2,1,0:T(8,128)}) %all-gather.2.cloned.1.call-update) | async-done | bytes 14155792 | tf_op jit(solution)/shard_map/all_gather | solution.py:51
  268.0 6.7 %reduce_sum.9 = f32[3,9,128,256]{3,2,1,0:T(8,128)S(1)} reduce(f32[4,3,9,128,256]{4,3,2,1,0:T(8,128)} %all-gather.2.cloned.1.call-done, f32[]{:T(128)} %constant.18.clone.1), dimensions={0}, to_apply=%region_1.2 | reduce | flops 2654208 | bytes 17694724 | tf_op jit(solution)/shard_map/reduce_sum | solution.py:51
  274.7 0.0 copy-start.1
  274.7 0.2 slice_bitcast_fusion.1
  274.9 0.1 collective-permute-start
  275.0 1.7 collective-permute-start.1
  276.8 13.9 %collective-permute-done = f32[9,128,256]{2,1,0:T(8,128)S(1)} collective-permute-done((f32[9,128,256]{2,1,0:T(8,128)S(1)}, f32[9,128,256]{2,1,0:T(8,128)S(1)}, u32[]{:S(2)}, u32[]{:S(2)}) %collective-permute-start) | collective-permute-done | bytes 1179680 | tf_op jit(solution)/shard_map/ppermute | solution.py:10
  290.6 0.0 collective-permute-done.1
  290.6 0.0 copy-done.1
  290.6 0.3 fusion.21
  291.0 1.7 collective-permute-start.2
  292.7 0.5 collective-permute-start.3
  293.2 7.5 %collective-permute-done.2 = bf16[1,9,128,256]{3,2,1,0:T(8,128)(2,1)S(1)} collective-permute-done((bf16[1,9,128,256]{3,2,1,0:T(8,128)(2,1)S(1)}, bf16[1,9,128,256]{3,2,1,0:T(8,128)(2,1)S(1)}, u32[]{:S(2)}, u32[]{:S(2)}) %collective-permute-start.2) | collective-permute-done | bytes 589856 | tf_op jit(solution)/shard_map/ppermute | solution.py:20
  300.7 0.0 collective-permute-done.3
  300.7 0.2 pad_maximum_fusion
  300.9 6.1 %gather_fusion.1 = bf16[96,128,256]{2,1,0:T(8,128)(2,1)} fusion(bf16[27,128,256]{2,1,0:T(8,128)(2,1)S(1)} %bitcast.65, s32[1024]{0:T(1024)S(1)} %pad_clamp_fusion), kind=kCustom, calls=%fused_computation.1 | custom fusion | bytes 12583296 | tf_op jit(solution)/shard_map/jit(_take)/gather | solution.py:57
  306.9 14.3 %broadcast_multiply_fusion = f32[96,256,256]{2,1,0:T(8,128)} fusion(f32[96]{0:T(128)S(1)} %get-tuple-element.7, bf16[1,1,96,256,128]{4,3,2,1,0:T(8,128)(2,1)} %param.7, bf16[96,128,256]{2,1,0:T(8,128)(2,1)} %gather_fusion.1, pred[96]{0:T(512)(128)(4,1)S(1)} %compare_and_fusion.1), kind=kOutput, calls=%fused_computation.7 | convolution fusion | flops 1620049920 | bytes 37749216 | tf_op jit(solution)/shard_map/krc,kcs->skr/dot_general | solution.py:58
  321.2 2.4 broadcast_in_dim.33
  323.7 54.3 %scatter_fusion.1 = f32[256,16,256]{2,0,1:T(8,128)} fusion(f32[256,16,256]{2,0,1:T(8,128)} %broadcast_in_dim.33, s32[96]{0:T(128)S(1)} %fusion.22, f32[96,256,256]{2,1,0:T(8,128)} %broadcast_multiply_fusion), kind=kCustom, calls=%fused_computation.3 | custom fusion | flops 6291456 | bytes 75497856 | tf_op jit(solution)/shard_map/scatter-add | solution.py:63
  377.9 2.4 convert_element_type.19
  380.4 2.4 copy.26
  382.7 3.4 copy.27
  386.1 68.2 %all_to_all.33 = bf16[256,8,512]{2,1,0:T(8,128)(2,1)S(1)} all-to-all(bf16[256,8,512]{2,1,0:T(8,128)(2,1)S(1)} %copy.27), channel_id=1, replica_groups=mesh['band'=4,'dom'=64] {'dom'}, dimensions={0} | all-to-all | bytes 4194304 | tf_op jit(solution)/shard_map/all_to_all | solution.py:66
  454.3 1.5 copy.32
  (6 shorter events, 0.0 us)
Async XLA Ops:
  6.5 17.5 %copy-start.2 = (s32[1,1,96]{2,1,0:T(1,128)S(1)}, s32[1,1,96]{2,1,0:T(1,128)}, u32[]{:S(2)}) copy-start(s32[1,1,96]{2,1,0:T(1,128)} %param.8) | copy-start | bytes 1156
  6.5 17.6 %copy-start.3 = (s32[1,1,96]{2,1,0:T(1,128)S(1)}, s32[1,1,96]{2,1,0:T(1,128)}, u32[]{:S(2)}) copy-start(s32[1,1,96]{2,1,0:T(1,128)} %param.9) | copy-start | bytes 1156
  11.1 63.4 %all-to-all-start = ((bf16[4,512,512]{2,0,1:T(4,128)(2,1)}), bf16[4,512,512]{2,0,1:T(4,128)(2,1)S(1)}, u32[]{:S(2)}, u32[]{:S(2)}) async-start(bf16[4,512,512]{2,0,1:T(4,128)(2,1)} %copy.21), calls=%async_computation | async-start | bytes 4194304 | tf_op jit(solution)/shard_map/all_to_all | solution.py:27
  23.2 244.8 %all-gather.2.cloned.1.call-start = ((), (), s32[]{:S(2)}) async-start(), calls=%async_computation.2 | async-start | bytes 17694720 | tf_op jit(solution)/shard_map/all_gather | solution.py:51
  135.4 1.7 copy-start
  274.7 15.9 %copy-start.1 = (f32[1152]{0:T(1024)S(1)}, f32[1152]{0:T(1024)}, u32[]{:S(2)}) copy-start(f32[1152]{0:T(1024)} %param.11) | copy-start | bytes 13828
  274.9 15.7 %collective-permute-start = (f32[9,128,256]{2,1,0:T(8,128)S(1)}, f32[9,128,256]{2,1,0:T(8,128)S(1)}, u32[]{:S(2)}, u32[]{:S(2)}) collective-permute-start(f32[9,128,256]{2,1,0:T(8,128)S(1)} %get-tuple-element.5), channel_id=1, source_target_pairs={{0,1},{1,2},{2,3},{3,4},{4,5},{5,6},{6,7},{7,8},{8,9},{9,10},{10,1... | collective-permute-start | bytes 3538952 | tf_op jit(solution)/shard_map/ppermute | solution.py:10
  275.0 15.6 %collective-permute-start.1 = (f32[9,128,256]{2,1,0:T(8,128)S(1)}, f32[9,128,256]{2,1,0:T(8,128)S(1)}, u32[]{:S(2)}, u32[]{:S(2)}) collective-permute-start(f32[9,128,256]{2,1,0:T(8,128)S(1)} %get-tuple-element.6), channel_id=1, source_target_pairs={{0,63},{1,0},{2,1},{3,2},{4,3},{5,4},{6,5},{7,6},{8,7},{9,8},{10,9... | collective-permute-start | bytes 3538952 | tf_op jit(solution)/shard_map/ppermute | solution.py:10
  291.0 9.7 %collective-permute-start.2 = (bf16[1,9,128,256]{3,2,1,0:T(8,128)(2,1)S(1)}, bf16[1,9,128,256]{3,2,1,0:T(8,128)(2,1)S(1)}, u32[]{:S(2)}, u32[]{:S(2)}) collective-permute-start(bf16[1,9,128,256]{3,2,1,0:T(8,128)(2,1)S(1)} %fusion.21), channel_id=1, source_target_pairs={{0,1},{1,2},{2,3},{3,4},{4,5},{5,6},{6,7},{7,8},{8,9},{9,10},{10,1... | collective-permute-start | bytes 1769480 | tf_op jit(solution)/shard_map/ppermute | solution.py:20
  292.7 8.0 %collective-permute-start.3 = (bf16[1,9,128,256]{3,2,1,0:T(8,128)(2,1)S(1)}, bf16[1,9,128,256]{3,2,1,0:T(8,128)(2,1)S(1)}, u32[]{:S(2)}, u32[]{:S(2)}) collective-permute-start(bf16[1,9,128,256]{3,2,1,0:T(8,128)(2,1)S(1)} %fusion.21), channel_id=1, source_target_pairs={{1,0},{2,1},{3,2},{4,3},{5,4},{6,5},{7,6},{8,7},{9,8},{10,9},{11,1... | collective-permute-start | bytes 1769480 | tf_op jit(solution)/shard_map/ppermute | solution.py:21
Sparse Core Ops, SparseCore 0:
  137.2 130.6 all-gather.1
